TPU v7x, 32 devices: a whole 2x2x4 slice. The times are simulated.
32 devices in a mesh: dp: 4 (over y, x), ctx: 8 (over z, core).
Axes of the slice: x: 2, y: 2, z: 4, core: 2. Of those that a mesh axis runs over, the one named last changes fastest.
Arguments:
- queries: bfloat16 [4096, 4096], P(('dp', 'ctx')), may hold values from -30 to 30
- key_input: bfloat16 [4096, 1024], P(('dp', 'ctx')), may hold values from -30 to 30
- value_input: bfloat16 [4096, 1024], P(('dp', 'ctx')), may hold values from -6 to 6
- out_grad: bfloat16 [4096, 4096], P(('dp', 'ctx')), may hold values from -6 to 6
- sink_logits: float32 [32], replicated, may hold values from 0 to 5
- doc_lengths: int32 [4, 4], replicated, may hold values from 1 to 4, 8 in all within a row
- assignment: int32 [4], replicated, may hold values from 0 to 3, each once
- stretch_map: int32 [16], replicated, may hold values from 0 to 15, each once
Outputs:
- attn_out: bfloat16 [4096, 4096], P(('dp', 'ctx'))
- query_grad: bfloat16 [4096, 4096], P(('dp', 'ctx'))
- key_grad: bfloat16 [4096, 1024], P(('dp', 'ctx'))
- value_grad: bfloat16 [4096, 1024], P(('dp', 'ctx'))
- sink_grad: float32 [32], replicated
Inputs may be any that keep to these rules, and one draw needn't show every extreme that they name: `doc_lengths`: lengths count blocks of 128 tokens; every row sums to 8 and its longest document has exactly 4 blocks. `assignment`: A permutation of the sequences. `stretch_map`: A permutation of the stretches, the same for every sequence.
All inputs are finite; a program needn't handle non-finite values.
Results may differ from a plain program's by a relative error of at most 0.019.
Values may be sent and summed in bfloat16 or wider, within the bound.
No kernel may reach another device: no remote copies, remote signals or barrier semaphores. Data moves between devices by JAX's collectives and lax.ppermute only.
A program may use at most 128 MiB of HBM per device.

v0:
```python
import jax
import jax.numpy as jnp
from jax import lax
from jax.sharding import PartitionSpec as P

HD = 128
BLOCK = 128


def true_positions(row_count, stretch_len, stretch_map):
    grid_shape = (row_count, stretch_map.shape[0])
    owners = lax.broadcasted_iota(jnp.int32, grid_shape, 0) // stretch_len
    picked = owners == lax.broadcasted_iota(jnp.int32, grid_shape, 1)
    leading = jnp.sum(jnp.where(picked, stretch_map[None, :], 0), axis=1)
    return leading * stretch_len + jnp.arange(row_count, dtype=jnp.int32) % stretch_len


def doc_numbers(positions, lengths):
    doc_ends = jnp.cumsum(lengths) * BLOCK
    return jnp.sum((positions[:, None] >= doc_ends[None, :]).astype(jnp.int32), axis=1)


def key_span():
    return 512


def visible(layout, first_row, block_rows):
    query_pos, query_doc, key_pos, key_doc = layout
    block_pos = lax.dynamic_slice_in_dim(key_pos, first_row, block_rows, 0)
    block_doc = lax.dynamic_slice_in_dim(key_doc, first_row, block_rows, 0)
    return (query_doc[:, None] == block_doc[None, :]) & (block_pos[None, :] <= query_pos[:, None])


def block_loop(row_count, advance, initial):
    block_rows = key_span()

    def one_turn(block_index, running):
        first_row = block_index * block_rows
        return advance(first_row, block_rows, running)

    return lax.fori_loop(0, row_count // block_rows, one_turn, initial)


def key_block(table, first_row, block_rows, query_heads):
    return lax.dynamic_slice_in_dim(table, first_row, block_rows, 0).reshape(
        block_rows, query_heads.shape[1], query_heads.shape[3]
    )


def block_scores(query_heads, key_table, first_row, block_rows, layout):
    key_rows = key_block(key_table, first_row, block_rows, query_heads)
    scores = jnp.einsum(
        "tgrd,ngd->tgrn", query_heads, key_rows, preferred_element_type=jnp.float32
    ) * HD ** (-0.5)
    allowed = visible(layout, first_row, block_rows)[:, None, None, :]
    return (scores, allowed, key_rows)


def block_weights(query_heads, key_table, first_row, block_rows, row_max, row_total, layout):
    scores, allowed, key_rows = block_scores(query_heads, key_table, first_row, block_rows, layout)
    weights = jnp.where(allowed, jnp.exp(scores - row_max[..., None]) / row_total[..., None], 0.0)
    return (weights, key_rows)


def softmax_stats(query_heads, key_table, sink_heads, layout):

    def advance(first_row, block_rows, running):
        row_max, row_total = running
        scores, allowed, key_rows = block_scores(
            query_heads, key_table, first_row, block_rows, layout
        )
        block_max = jnp.max(jnp.where(allowed, scores, -jnp.inf), axis=3)
        fresh_max = jnp.maximum(row_max, block_max)
        exp_terms = jnp.where(allowed, jnp.exp(scores - fresh_max[..., None]), 0.0)
        return (fresh_max, row_total * jnp.exp(row_max - fresh_max) + jnp.sum(exp_terms, axis=3))

    start_max = jnp.broadcast_to(sink_heads[None], query_heads.shape[:3])
    start_total = jnp.ones(query_heads.shape[:3], jnp.float32)
    return block_loop(key_table.shape[0], advance, (start_max, start_total))


def attend_values(query_heads, key_table, value_table, row_max, row_total, layout):

    def advance(first_row, block_rows, partial_value):
        weights, key_rows = block_weights(
            query_heads, key_table, first_row, block_rows, row_max, row_total, layout
        )
        value_rows = key_block(value_table, first_row, block_rows, query_heads)
        return partial_value + jnp.einsum(
            "tgrn,ngd->tgrd",
            weights.astype(jnp.bfloat16),
            value_rows,
            preferred_element_type=jnp.float32,
        )

    return block_loop(key_table.shape[0], advance, jnp.zeros(query_heads.shape, jnp.float32))


def backward_block(
    query_heads, grad_heads, key_table, value_table, row_stats, layout, first_row, block_rows
):
    row_max, row_total, row_dot = row_stats
    weights, key_rows = block_weights(
        query_heads, key_table, first_row, block_rows, row_max, row_total, layout
    )
    value_rows = key_block(value_table, first_row, block_rows, query_heads)
    grad_weights = jnp.einsum(
        "tgrd,ngd->tgrn", grad_heads, value_rows, preferred_element_type=jnp.float32
    )
    grad_scores = (weights * (grad_weights - row_dot[..., None]) * HD ** (-0.5)).astype(
        jnp.bfloat16
    )
    return (weights.astype(jnp.bfloat16), grad_scores, key_rows)


def query_grads(query_heads, grad_heads, key_table, value_table, row_stats, layout):

    def advance(first_row, block_rows, partial_value):
        weights_b, grad_scores, key_rows = backward_block(
            query_heads,
            grad_heads,
            key_table,
            value_table,
            row_stats,
            layout,
            first_row,
            block_rows,
        )
        return partial_value + jnp.einsum(
            "tgrn,ngd->tgrd", grad_scores, key_rows, preferred_element_type=jnp.float32
        )

    return block_loop(key_table.shape[0], advance, jnp.zeros(query_heads.shape, jnp.float32))


def key_grads(query_heads, grad_heads, key_table, value_table, row_stats, layout):
    grad_shape = (key_table.shape[0], query_heads.shape[1], query_heads.shape[3])

    def advance(first_row, block_rows, running):
        key_sum, value_sum = running
        weights_b, grad_scores, key_rows = backward_block(
            query_heads,
            grad_heads,
            key_table,
            value_table,
            row_stats,
            layout,
            first_row,
            block_rows,
        )
        key_part = jnp.einsum(
            "tgrn,tgrd->ngd", grad_scores, query_heads, preferred_element_type=jnp.float32
        )
        value_part = jnp.einsum(
            "tgrn,tgrd->ngd", weights_b, grad_heads, preferred_element_type=jnp.float32
        )
        return (
            lax.dynamic_update_slice_in_dim(key_sum, key_part, first_row, 0),
            lax.dynamic_update_slice_in_dim(value_sum, value_part, first_row, 0),
        )

    initial = (jnp.zeros(grad_shape, jnp.float32), jnp.zeros(grad_shape, jnp.float32))
    return block_loop(key_table.shape[0], advance, initial)


def per_device(
    queries, key_input, value_input, out_grad, sink_logits, doc_lengths, assignment, stretch_map
):
    local_rows = queries.shape[0]
    ctx_size = lax.axis_size("ctx")
    seq_rows = local_rows * ctx_size
    head_count = sink_logits.shape[0]
    kv_heads = key_input.shape[1] // HD
    group_size = head_count // kv_heads
    group_index = lax.axis_index("dp")
    place_index = lax.axis_index("ctx")
    sequence_ids = jnp.arange(doc_lengths.shape[0], dtype=jnp.int32)
    chosen = jnp.sum(jnp.where(sequence_ids == group_index, assignment, 0))
    lengths = jnp.sum(jnp.where((sequence_ids == chosen)[:, None], doc_lengths, 0), axis=0)
    positions = true_positions(seq_rows, local_rows // 2, stretch_map)
    documents = doc_numbers(positions, lengths)
    whole_keys, whole_values = (
        lax.all_gather(key_input, "ctx", axis=0, tiled=True),
        lax.all_gather(value_input, "ctx", axis=0, tiled=True),
    )
    query_heads = queries.reshape(local_rows, kv_heads, group_size, HD)
    grad_heads = out_grad.reshape(local_rows, kv_heads, group_size, HD)
    sink_heads = sink_logits.reshape(kv_heads, group_size)
    query_pos = lax.dynamic_slice_in_dim(positions, place_index * local_rows, local_rows, 0)
    query_doc = lax.dynamic_slice_in_dim(documents, place_index * local_rows, local_rows, 0)
    layout = (query_pos, query_doc, positions, documents)
    row_max, row_total = softmax_stats(query_heads, whole_keys, sink_heads, layout)
    attn_heads = attend_values(
        query_heads, whole_keys, whole_values, row_max, row_total, layout
    ).astype(jnp.bfloat16)
    row_dot = jnp.sum(grad_heads.astype(jnp.float32) * attn_heads.astype(jnp.float32), axis=3)
    partial_sink = (
        -jnp.sum(jnp.exp(sink_heads[None] - row_max) / row_total * row_dot, axis=0)
    ).reshape(head_count)
    row_stats = (row_max, row_total, row_dot)
    query_sum = query_grads(query_heads, grad_heads, whole_keys, whole_values, row_stats, layout)
    local_layout = (query_pos, query_doc, positions, documents)
    key_sum, value_sum = key_grads(
        query_heads, grad_heads, whole_keys, whole_values, row_stats, local_layout
    )
    summed = lax.psum_scatter(
        jnp.stack(
            (
                key_sum.reshape(lax.axis_size("ctx") * local_rows, -1),
                value_sum.reshape(lax.axis_size("ctx") * local_rows, -1),
            ),
            axis=1,
        ),
        "ctx",
        scatter_dimension=0,
        tiled=True,
    )
    attn_out = attn_heads.reshape(local_rows, head_count * HD)
    query_grad = query_sum.astype(jnp.bfloat16).reshape(local_rows, head_count * HD)
    key_grad = summed[:, 0, :].astype(jnp.bfloat16)
    value_grad = summed[:, 1, :].astype(jnp.bfloat16)
    sink_grad = lax.psum(partial_sink, ("dp", "ctx"))
    return (attn_out, query_grad, key_grad, value_grad, sink_grad)


def solution(mesh):
    placed = (
        P(("dp", "ctx"), None),
        P(("dp", "ctx"), None),
        P(("dp", "ctx"), None),
        P(("dp", "ctx"), None),
        P(),
        P(),
        P(),
        P(),
    )
    return jax.shard_map(
        per_device,
        mesh=mesh,
        in_specs=placed,
        out_specs=(
            P(("dp", "ctx"), None),
            P(("dp", "ctx"), None),
            P(("dp", "ctx"), None),
            P(("dp", "ctx"), None),
            P(),
        ),
        check_vma=False,
    )
```

profile of v0, /device:TPU:0, one launch (start us, length us, event | category | flops | bytes accessed | tf_op | source)
XLA Modules:
  0.0 268.9 jit_solution(8948219369799919933)
XLA Ops:
  7.2 1.9 copy.93
  9.2 1.8 copy.92
  11.1 0.7 select_reduce_fusion
  11.9 1.3 fusion.60
  13.1 0.6 iota_compare_fusion.1
  13.8 0.8 select_reduce_fusion.1
  15.0 1.6 copy.94
  16.6 0.7 copy.97
  17.4 0.7 copy.98
  18.1 1.3 copy.101
  19.4 24.4 %all-gather.5.cloned.1.call-done = bf16[1024,1024]{0,1:T(8,128)(2,1)} async-done(((bf16[128,1024]{0,1:T(8,128)(2,1)}), bf16[1024,1024]{0,1:T(8,128)(2,1)}) %all-gather.5.cloned.1.call-update) | async-done | bytes 2097168 | tf_op jit(solution)/shard_map/all_gather | solution.py:183
  43.8 10.1 %while.60 = (s32[]{:T(128)}, f32[128,8,4]{0,2,1:T(4,128)S(1)}, f32[128,8,4]{0,2,1:T(4,128)S(1)}, s32[128]{0:T(128)S(1)}, s32[1024]{0:T(1024)S(1)}, /*index=5*/s3...) while((s32[]{:T(128)}, f32[128,8,4]{0,2,1:T(4,128)S(1)}, ...), condition=%wide.region_8.9_spmd.clone, body=%wide.region_5.8_spmd.clone.sunk | while | flops 551759872 | bytes 21394624 | solution.py:41
  44.2 1.3 constant_dynamic-slice_fusion.14
  45.5 1.5 fusion.118
  47.0 1.8 fusion.119
  49.3 1.3 constant_dynamic-slice_fusion.14
  50.6 1.5 fusion.118
  52.0 1.8 fusion.119
  53.9 21.9 %all-gather.3.cloned.1.call-done = bf16[1024,1024]{0,1:T(8,128)(2,1)} async-done(((bf16[128,1024]{0,1:T(8,128)(2,1)}), bf16[1024,1024]{0,1:T(8,128)(2,1)}) %all-gather.3.cloned.1.call-update) | async-done | bytes 2097168 | tf_op jit(solution)/shard_map/all_gather | solution.py:184
  75.9 13.1 %while.61 = (s32[]{:T(128)}, f32[128,8,4,128]{0,3,2,1:T(8,128)}, bf16[1024,1024]{0,1:T(8,128)(2,1)}, s32[128]{0:T(128)S(1)}, s32[1024]{0:T(1024)S(1)}, /*index=5...) while((s32[]{:T(128)}, f32[128,8,4,128]{0,3,2,1:T(8,128)}, ...), condition=%wide.region_10.11_spmd.clone, body=%wide.region_9.10_spmd.clone.sunk | while | flops 1085472768 | bytes 11711697 | solution.py:41
  76.2 1.7 constant_dynamic-slice_fusion.15
  77.9 3.9 %bitcast_add_fusion.4 = f32[128,8,4,128]{0,3,2,1:T(8,128)} fusion(f32[128,8,4,128]{0,3,2,1:T(8,128)} %get-tuple-element.1586, bf16[512,8,128,1]{0,2,3,1:T(8,128)(2,1)S(1)} %bitcast.221, f32[128,8,4]{0,2,1:T(4,128)S(1)} %get-tuple-element.1610, f32[128,8,4]{0,2,1:T(4,128)S(1)} %get-tuple-element.1609, pred[128,512]{0,1:T(8,128)(4,1)S(1)} %compare_and_fusion.10, ...), kind=kOutput, calls=%fused_computation.39.clone.1 | convolution fusion | flops 1085276160 | bytes 7438337 | tf_op jit(solution)/shard_map/while/body/eval_jaxpr/tgrn,ngd->tgrd/dot_general | solution.py:89
  82.2 1.7 constant_dynamic-slice_fusion.15
  83.9 5.1 %bitcast_add_fusion.4 = f32[128,8,4,128]{0,3,2,1:T(8,128)} fusion(f32[128,8,4,128]{0,3,2,1:T(8,128)} %get-tuple-element.1586, bf16[512,8,128,1]{0,2,3,1:T(8,128)(2,1)S(1)} %bitcast.221, f32[128,8,4]{0,2,1:T(4,128)S(1)} %get-tuple-element.1610, f32[128,8,4]{0,2,1:T(4,128)S(1)} %get-tuple-element.1609, pred[128,512]{0,1:T(8,128)(4,1)S(1)} %compare_and_fusion.10, ...), kind=kOutput, calls=%fused_computation.39.clone.1 | convolution fusion | flops 1085276160 | bytes 7438337 | tf_op jit(solution)/shard_map/while/body/eval_jaxpr/tgrn,ngd->tgrd/dot_general | solution.py:89
  89.0 3.3 %multiply_reduce_fusion = (f32[128,8,4]{0,2,1:T(4,128)S(1)}, bf16[128,8,4,128]{0,3,2,1:T(8,128)(2,1)}) fusion(bf16[128,4096]{0,1:T(8,128)(2,1)} %copy-done.8, f32[128,8,4,128]{0,3,2,1:T(8,128)} %get-tuple-element.790), kind=kLoop, calls=%fused_computation.62 | loop fusion | flops 2617344 | bytes 4210688 | tf_op jit(solution)/shard_map/reduce_sum | solution.py:196
  92.3 2.4 broadcast.265.clone
  94.6 2.3 broadcast.265.clone2
  96.9 55.1 %while.59 = (s32[]{:T(128)}, f32[1024,8,128]{2,1,0:T(8,128)}, f32[1024,8,128]{2,1,0:T(8,128)}, s32[128]{0:T(128)S(1)}, s32[1024]{0:T(1024)S(1)}, /*index=5*/s32[...) while((s32[]{:T(128)}, f32[1024,8,128]{2,1,0:T(8,128)}, ...), condition=%wide.region_15.16_spmd, body=%wide.region_14.15_spmd.sunk | while | flops 2166554624 | bytes 132314512 | solution.py:41
  97.4 4.5 %fusion.113 = f32[128,8,4,512]{0,3,2,1:T(8,128)} fusion(f32[128,8,4]{0,2,1:T(4,128)S(1)} %get-tuple-element.1712, f32[128,8,4]{0,2,1:T(4,128)S(1)} %get-tuple-element.1711, pred[128,512]{0,1:T(8,128)(4,1)S(1)} %compare_and_fusion.8, bf16[512,8,128,1]{0,2,3,1:T(8,128)(2,1)S(1)} %bitcast.222, bf16[128,8,4,128]{3,0,2,1:T(8,128)(2,1)S(1)} %get-tuple-element.1710), kind=kOutput, calls=%fused_computation.7.clone.1 | convolution fusion | flops 545259520 | bytes 10584064 | tf_op jit(solution)/shard_map/while/body/eval_jaxpr/tgrd,ngd->tgrn/dot_general | solution.py:52
  101.9 1.1 constant_dynamic-slice_fusion.13
  103.0 7.8 %fusion.115 = f32[512,8,128]{2,0,1:T(8,128)} fusion(bf16[128,8,4,128]{3,0,2,1:T(8,128)(2,1)S(1)} %get-tuple-element.1710, f32[128,8,4,512]{0,3,2,1:T(8,128)} %fusion.113, f32[128,8,4]{0,2,1:T(4,128)S(1)} %get-tuple-element.1715, bf16[512,8,128,1]{0,2,3,1:T(8,128)(2,1)} %bitcast.218, bf16[128,8,4,128]{3,0,2,1:T(8,128)(2,1)} %get-tuple-element.1714), kind=kOutput, calls=%fused_computation.17.clone.1 | convolution fusion | flops 1082130432 | bytes 13647872 | tf_op jit(solution)/shard_map/while/body/eval_jaxpr/tgrn,tgrd->ngd/dot_general | solution.py:151
  110.8 5.0 %fusion.114 = f32[512,8,128]{2,0,1:T(8,128)S(1)} fusion(bf16[128,8,4,128]{3,0,2,1:T(8,128)(2,1)} %get-tuple-element.1714, f32[128,8,4,512]{0,3,2,1:T(8,128)} %fusion.113), kind=kOutput, calls=%fused_computation.16.clone.1 | convolution fusion | flops 538968064 | bytes 11534336 | tf_op jit(solution)/shard_map/while/body/eval_jaxpr/tgrn,tgrd->ngd/dot_general | solution.py:154
  116.3 1.2 copy-done.6
  117.5 2.9 %copy_dynamic-update-slice_fusion.3 = (f32[1024,8,128]{2,1,0:T(8,128)S(1)}, f32[1024,8,128]{2,1,0:T(8,128)S(1)}) fusion(f32[1024,8,128]{2,1,0:T(8,128)S(1)} %copy-done.6, s32[]{:T(128)S(6)} %select_n.162, f32[512,8,128]{2,0,1:T(8,128)S(1)} %fusion.114, f32[1024,8,128]{2,1,0:T(8,128)S(1)} %copy-done.4, f32[512,8,128]{2,0,1:T(8,128)S(1)} %copy-done.1), kind=kLoop, calls=%fused_computation.14.clone.1 | loop fusion | bytes 8388612 | tf_op jit(solution)/shard_map/while/body/eval_jaxpr/dynamic_update_slice | solution.py:159
  120.4 2.1 copy-done.5
  122.5 2.0 copy-done.7
  124.9 4.5 %fusion.113 = f32[128,8,4,512]{0,3,2,1:T(8,128)} fusion(f32[128,8,4]{0,2,1:T(4,128)S(1)} %get-tuple-element.1712, f32[128,8,4]{0,2,1:T(4,128)S(1)} %get-tuple-element.1711, pred[128,512]{0,1:T(8,128)(4,1)S(1)} %compare_and_fusion.8, bf16[512,8,128,1]{0,2,3,1:T(8,128)(2,1)S(1)} %bitcast.222, bf16[128,8,4,128]{3,0,2,1:T(8,128)(2,1)S(1)} %get-tuple-element.1710), kind=kOutput, calls=%fused_computation.7.clone.1 | convolution fusion | flops 545259520 | bytes 10584064 | tf_op jit(solution)/shard_map/while/body/eval_jaxpr/tgrd,ngd->tgrn/dot_general | solution.py:52
  129.5 1.1 constant_dynamic-slice_fusion.13
  130.5 7.8 %fusion.115 = f32[512,8,128]{2,0,1:T(8,128)} fusion(bf16[128,8,4,128]{3,0,2,1:T(8,128)(2,1)S(1)} %get-tuple-element.1710, f32[128,8,4,512]{0,3,2,1:T(8,128)} %fusion.113, f32[128,8,4]{0,2,1:T(4,128)S(1)} %get-tuple-element.1715, bf16[512,8,128,1]{0,2,3,1:T(8,128)(2,1)} %bitcast.218, bf16[128,8,4,128]{3,0,2,1:T(8,128)(2,1)} %get-tuple-element.1714), kind=kOutput, calls=%fused_computation.17.clone.1 | convolution fusion | flops 1082130432 | bytes 13647872 | tf_op jit(solution)/shard_map/while/body/eval_jaxpr/tgrn,tgrd->ngd/dot_general | solution.py:151
  138.3 5.0 %fusion.114 = f32[512,8,128]{2,0,1:T(8,128)S(1)} fusion(bf16[128,8,4,128]{3,0,2,1:T(8,128)(2,1)} %get-tuple-element.1714, f32[128,8,4,512]{0,3,2,1:T(8,128)} %fusion.113), kind=kOutput, calls=%fused_computation.16.clone.1 | convolution fusion | flops 538968064 | bytes 11534336 | tf_op jit(solution)/shard_map/while/body/eval_jaxpr/tgrn,tgrd->ngd/dot_general | solution.py:154
  143.8 1.2 copy-done.6
  145.1 2.9 %copy_dynamic-update-slice_fusion.3 = (f32[1024,8,128]{2,1,0:T(8,128)S(1)}, f32[1024,8,128]{2,1,0:T(8,128)S(1)}) fusion(f32[1024,8,128]{2,1,0:T(8,128)S(1)} %copy-done.6, s32[]{:T(128)S(6)} %select_n.162, f32[512,8,128]{2,0,1:T(8,128)S(1)} %fusion.114, f32[1024,8,128]{2,1,0:T(8,128)S(1)} %copy-done.4, f32[512,8,128]{2,0,1:T(8,128)S(1)} %copy-done.1), kind=kLoop, calls=%fused_computation.14.clone.1 | loop fusion | bytes 8388612 | tf_op jit(solution)/shard_map/while/body/eval_jaxpr/dynamic_update_slice | solution.py:159
  147.9 2.1 copy-done.5
  150.0 2.0 copy-done.7
  152.0 4.9 %stack_reshape.6 = f32[1024,1,1024]{2,0,1:T(8,128)} reshape(f32[1024,8,128]{2,1,0:T(8,128)} %get-tuple-element.792) | data formatting | bytes 8388608 | tf_op jit(solution)/shard_map/stack;reshape | solution.py:207
  156.9 4.9 %stack_reshape.7 = f32[1024,1,1024]{2,0,1:T(8,128)} reshape(f32[1024,8,128]{2,1,0:T(8,128)} %get-tuple-element.793) | data formatting | bytes 8388608 | tf_op jit(solution)/shard_map/stack;reshape | solution.py:207
  161.8 8.5 %pad_maximum_fusion = f32[1024,2,1024]{2,0,1:T(8,128)} fusion(f32[1024,1,1024]{2,0,1:T(8,128)} %stack_reshape.7, f32[1024,1,1024]{2,0,1:T(8,128)} %stack_reshape.6), kind=kLoop, calls=%fused_computation.61 | loop fusion | flops 2097152 | bytes 16777216 | tf_op jit(solution)/shard_map/stack | solution.py:207
  170.3 1.1 copy.141
  171.5 1.0 copy.110
  172.5 1.3 multiply_reduce_fusion.1
  173.9 42.8 %psum.7 = f32[32]{0:T(128)} all-reduce(f32[32]{0:T(128)S(1)} %neg.8), channel_id=1, replica_groups=mesh['dp'=4,'ctx'=8] {'dp','ctx'}, use_global_device_ids=true, to_apply=%region_18.19 | all-reduce | flops 32 | bytes 256 | tf_op jit(solution)/shard_map/psum | solution.py:222
  216.8 34.3 %while.62 = (s32[]{:T(128)}, f32[128,8,4,128]{0,3,2,1:T(8,128)}, bf16[1024,1024]{0,1:T(8,128)(2,1)S(1)}, s32[128]{0:T(128)S(1)}, s32[1024]{0:T(1024)S(1)}, /*ind...) while((s32[]{:T(128)}, f32[128,8,4,128]{0,3,2,1:T(8,128)}, ...), condition=%wide.region_13.14_spmd.clone, body=%wide.region_12.13_spmd.clone.sunk | while | flops 1628635136 | bytes 34796796 | solution.py:41
  217.1 2.4 constant_dynamic-slice_fusion.16
  219.5 4.6 %fusion.131 = f32[8,512,128,4]{2,1,3,0:T(8,128)} fusion(bf16[512,8,128,1]{0,2,3,1:T(8,128)(2,1)S(1)} %bitcast.215, bf16[128,8,4,128]{3,0,2,1:T(8,128)(2,1)S(1)} %get-tuple-element.1656), kind=kOutput, calls=%fused_computation.87.clone.1 | convolution fusion | flops 536870912 | bytes 10485760 | tf_op jit(solution)/shard_map/while/body/eval_jaxpr/tgrd,ngd->tgrn/dot_general | solution.py:52
  224.1 9.5 %bitcast_add_fusion.5 = f32[128,8,4,128]{0,3,2,1:T(8,128)} fusion(f32[128,8,4,128]{0,3,2,1:T(8,128)} %get-tuple-element.1633, bf16[512,8,128,1]{0,2,3,1:T(8,128)(2,1)} %bitcast.216, f32[8,512,128,4]{2,1,3,0:T(8,128)} %fusion.131, f32[128,8,4]{0,2,1:T(4,128)S(1)} %get-tuple-element.1661, f32[128,8,4]{0,2,1:T(4,128)S(1)} %get-tuple-element.1658, ...), kind=kOutput, calls=%fused_computation.55.clone.1 | convolution fusion | flops 1091567616 | bytes 15843329 | tf_op jit(solution)/shard_map/while/body/eval_jaxpr/tgrn,ngd->tgrd/dot_general | solution.py:129
  234.0 2.4 constant_dynamic-slice_fusion.16
  236.4 4.6 %fusion.131 = f32[8,512,128,4]{2,1,3,0:T(8,128)} fusion(bf16[512,8,128,1]{0,2,3,1:T(8,128)(2,1)S(1)} %bitcast.215, bf16[128,8,4,128]{3,0,2,1:T(8,128)(2,1)S(1)} %get-tuple-element.1656), kind=kOutput, calls=%fused_computation.87.clone.1 | convolution fusion | flops 536870912 | bytes 10485760 | tf_op jit(solution)/shard_map/while/body/eval_jaxpr/tgrd,ngd->tgrn/dot_general | solution.py:52
  241.0 10.1 %bitcast_add_fusion.5 = f32[128,8,4,128]{0,3,2,1:T(8,128)} fusion(f32[128,8,4,128]{0,3,2,1:T(8,128)} %get-tuple-element.1633, bf16[512,8,128,1]{0,2,3,1:T(8,128)(2,1)} %bitcast.216, f32[8,512,128,4]{2,1,3,0:T(8,128)} %fusion.131, f32[128,8,4]{0,2,1:T(4,128)S(1)} %get-tuple-element.1661, f32[128,8,4]{0,2,1:T(4,128)S(1)} %get-tuple-element.1658, ...), kind=kOutput, calls=%fused_computation.55.clone.1 | convolution fusion | flops 1091567616 | bytes 15843329 | tf_op jit(solution)/shard_map/while/body/eval_jaxpr/tgrn,ngd->tgrd/dot_general | solution.py:129
  251.1 1.9 convert_element_type.55
  253.0 1.3 copy.128
  254.3 1.3 copy.111
  255.6 4.6 %reduce-scatter.2.cloned.1.call-done = f32[128,2,1024]{2,0,1:T(8,128)} async-done(((f32[1024,2,1024]{2,0,1:T(8,128)}), f32[128,2,1024]{2,0,1:T(8,128)}) %reduce-scatter.2.cloned.1.call-update) | async-done | bytes 1048592 | tf_op jit(solution)/shard_map/reduce_scatter | solution.py:206
  260.2 1.3 convert.4
  261.5 0.8 slice_bitcast_fusion
  (90 shorter events, 5.1 us)
Async XLA Ops:
  7.2 10.1 %copy-start.13 = (f32[32]{0:T(128)S(1)}, f32[32]{0:T(128)}, u32[]{:S(2)}) copy-start(f32[32]{0:T(128)} %param.20) | copy-start | bytes 388
  7.2 10.2 %copy-start.10 = (bf16[128,4096]{1,0:T(8,128)(2,1)S(1)}, bf16[128,4096]{1,0:T(8,128)(2,1)}, u32[]{:S(2)}) copy-start(bf16[128,4096]{1,0:T(8,128)(2,1)} %param.19) | copy-start | bytes 3145732
  7.2 36.6 %all-gather.5.cloned.1.call-start = ((), (), s32[]{:S(2)}) async-start(), calls=%async_computation.2 | async-start | bytes 2359296 | tf_op jit(solution)/shard_map/all_gather | solution.py:183
  9.1 66.7 %all-gather.3.cloned.1.call-start = ((), (), s32[]{:S(2)}) async-start(), calls=%async_computation.1 | async-start | bytes 2359296 | tf_op jit(solution)/shard_map/all_gather | solution.py:184
  11.0 249.2 %reduce-scatter.2.cloned.1.call-start = ((), (), s32[]{:S(2)}) async-start(), calls=%async_computation.3 | async-start | bytes 9437184 | tf_op jit(solution)/shard_map/reduce_scatter | solution.py:206
  17.4 26.4 %copy-start.11 = (f32[8,4]{1,0:T(8,128)}, f32[8,4]{1,0:T(8,128)S(1)}, u32[]{:S(2)}) copy-start(f32[8,4]{1,0:T(8,128)S(1)} %broadcast_in_dim.233) | copy-start | bytes 388
  18.0 25.8 %copy-start.8 = (bf16[128,4096]{0,1:T(8,128)(2,1)}, bf16[128,4096]{0,1:T(8,128)(2,1)S(1)}, u32[]{:S(2)}) copy-start(bf16[128,4096]{0,1:T(8,128)(2,1)S(1)} %copy.98) | copy-start | bytes 3145732
  92.3 4.6 %copy-start = (bf16[1024,1024]{0,1:T(8,128)(2,1)S(1)}, bf16[1024,1024]{0,1:T(8,128)(2,1)}, u32[]{:S(2)}) copy-start(bf16[1024,1024]{0,1:T(8,128)(2,1)} %get-tuple-element.1728) | copy-start | bytes 6291460
  97.4 4.5 %copy-start.2 = (bf16[1024,1024]{0,1:T(8,128)(2,1)S(1)}, bf16[1024,1024]{0,1:T(8,128)(2,1)}, u32[]{:S(2)}) copy-start(bf16[1024,1024]{0,1:T(8,128)(2,1)} %get-tuple-element.1713) | copy-start | bytes 6291460 | tf_op jit(solution)/shard_map/while
  110.8 5.0 %copy-start.1 = (f32[512,8,128]{2,0,1:T(8,128)S(1)}, f32[512,8,128]{2,0,1:T(8,128)}, u32[]{:S(2)}) copy-start(f32[512,8,128]{2,0,1:T(8,128)} %fusion.115) | copy-start | bytes 6291460 | tf_op jit(solution)/shard_map/while
  110.8 5.5 %copy-start.4 = (f32[1024,8,128]{2,1,0:T(8,128)S(1)}, f32[1024,8,128]{2,1,0:T(8,128)}, u32[]{:S(2)}) copy-start(f32[1024,8,128]{2,1,0:T(8,128)} %get-tuple-element.1685) | copy-start | bytes 12582916 | tf_op jit(solution)/shard_map/while
  110.8 6.7 %copy-start.6 = (f32[1024,8,128]{2,1,0:T(8,128)S(1)}, f32[1024,8,128]{2,1,0:T(8,128)}, u32[]{:S(2)}) copy-start(f32[1024,8,128]{2,1,0:T(8,128)} %get-tuple-element.1686) | copy-start | bytes 12582916 | tf_op jit(solution)/shard_map/while
  120.4 2.1 copy-start.5
  122.5 2.0 copy-start.7
  124.9 4.5 %copy-start.2 = (bf16[1024,1024]{0,1:T(8,128)(2,1)S(1)}, bf16[1024,1024]{0,1:T(8,128)(2,1)}, u32[]{:S(2)}) copy-start(bf16[1024,1024]{0,1:T(8,128)(2,1)} %get-tuple-element.1713) | copy-start | bytes 6291460 | tf_op jit(solution)/shard_map/while
  138.3 5.0 %copy-start.1 = (f32[512,8,128]{2,0,1:T(8,128)S(1)}, f32[512,8,128]{2,0,1:T(8,128)}, u32[]{:S(2)}) copy-start(f32[512,8,128]{2,0,1:T(8,128)} %fusion.115) | copy-start | bytes 6291460 | tf_op jit(solution)/shard_map/while
  138.3 5.5 %copy-start.4 = (f32[1024,8,128]{2,1,0:T(8,128)S(1)}, f32[1024,8,128]{2,1,0:T(8,128)}, u32[]{:S(2)}) copy-start(f32[1024,8,128]{2,1,0:T(8,128)} %get-tuple-element.1685) | copy-start | bytes 12582916 | tf_op jit(solution)/shard_map/while
  138.3 6.7 %copy-start.6 = (f32[1024,8,128]{2,1,0:T(8,128)S(1)}, f32[1024,8,128]{2,1,0:T(8,128)}, u32[]{:S(2)}) copy-start(f32[1024,8,128]{2,1,0:T(8,128)} %get-tuple-element.1686) | copy-start | bytes 12582916 | tf_op jit(solution)/shard_map/while
  147.9 2.1 copy-start.5
  150.0 2.0 copy-start.7
  170.3 1.1 copy-start.12
  219.5 4.6 %copy-start.3 = (bf16[512,1024]{0,1:T(8,128)(2,1)}, bf16[512,1024]{0,1:T(8,128)(2,1)S(1)}, u32[]{:S(2)}) copy-start(bf16[512,1024]{0,1:T(8,128)(2,1)S(1)} %get-tuple-element.1529) | copy-start | bytes 3145732 | tf_op jit(solution)/shard_map/while
  236.4 4.6 %copy-start.3 = (bf16[512,1024]{0,1:T(8,128)(2,1)}, bf16[512,1024]{0,1:T(8,128)(2,1)S(1)}, u32[]{:S(2)}) copy-start(bf16[512,1024]{0,1:T(8,128)(2,1)S(1)} %get-tuple-element.1529) | copy-start | bytes 3145732 | tf_op jit(solution)/shard_map/while
  251.1 3.2 %copy-start.9 = (bf16[128,8,4,128]{0,3,2,1:T(8,128)(2,1)S(1)}, bf16[128,8,4,128]{0,3,2,1:T(8,128)(2,1)}, u32[]{:S(2)}) copy-start(bf16[128,8,4,128]{0,3,2,1:T(8,128)(2,1)} %get-tuple-element.1216) | copy-start | bytes 3145732
Sparse Core Ops, SparseCore 0:
  10.2 33.5 all-gather.4
  45.9 29.8 all-gather.2
  170.5 89.7 reduce-scatter.1
where the time goes:
time: 270 us; the launch traced here: 269 us
  matrix products  75.3 us (28%)
  local copies, waits for them, and re-layouts  59.9 us (22%)
  waiting for transfers between devices  51 us (19%)
  blocking collectives  42.8 us (16%)
  other arithmetic  25.6 us (9%)
  between operations  13.9 us (5%)
    psum x1, blocking collectives, per_device(): sink_grad = lax.psum(partial_sink, ('dp', 'ctx'))  42.8 us
    all_gather x1, waiting for transfers between devices, per_device(): lax.all_gather(key_input, 'ctx', axis=0, tiled=True)  24.4 us
    all_gather x1, waiting for transfers between devices, per_device(): lax.all_gather(value_input, 'ctx', axis=0, tiled=True)  21.9 us
    dot_general x6, matrix products, block_scores(): jnp.einsum('tgrd,ngd->tgrn', query_heads, key_rows, preferred_element_typ...  21.1 us
    dot_general x2, matrix products, advance(): jnp.einsum('tgrn,ngd->tgrd', grad_scores, key_rows, preferred_element_typ...  19.6 us
    dot_general x2, matrix products, advance(): jnp.einsum('tgrn,tgrd->ngd', grad_scores, query_heads, preferred_element_...  15.6 us
    dynamic_slice x10, local copies, waits for them, and re-layouts, key_block(): lax.dynamic_slice_in_dim(table, first_row, block_rows, 0)  13.2 us
    while x30, local copies, waits for them, and re-layouts  11.6 us
  transfers between devices with their start and end apart: 3, of which 3 were waited for; matrix products, arithmetic and copies ran while one was open for 23% of the time, Pallas kernels for 0%

commit v1 on v0

--- a/solution.py
+++ b/solution.py
@@ -5,6 +5,28 @@
 
 HD = 128
 BLOCK = 128
+
+
+def laid_out(parts, dim):
+    parts = jnp.moveaxis(parts, 0, dim)
+    shape = parts.shape
+    return parts.reshape(*shape[:dim], shape[dim] * shape[dim + 1], *shape[dim + 2 :])
+
+
+def ring_gather(shard, axis, dim):
+    size = lax.axis_size(axis)
+    pairs = [(i, (i + 1) % size) for i in range(size)]
+    back = [(b, a) for a, b in pairs]
+    lower, upper = ([], [])
+    for hop in range(size - 1):
+        if hop % 2 == 0:
+            lower.append(lax.ppermute(lower[-1] if lower else shard, axis, pairs))
+        else:
+            upper.append(lax.ppermute(upper[-1] if upper else shard, axis, back))
+    blocks = jnp.stack([*lower[::-1], shard, *upper])
+    shift = lax.axis_index(axis) - len(lower)
+    blocks = blocks[(jnp.arange(size) - shift) % size]
+    return laid_out(blocks, dim)
 
 
 def true_positions(row_count, stretch_len, stretch_map):
@@ -180,7 +202,7 @@
     positions = true_positions(seq_rows, local_rows // 2, stretch_map)
     documents = doc_numbers(positions, lengths)
     whole_keys, whole_values = (
-        lax.all_gather(key_input, "ctx", axis=0, tiled=True),
+        ring_gather(key_input, "ctx", 0),
         lax.all_gather(value_input, "ctx", axis=0, tiled=True),
     )
     query_heads = queries.reshape(local_rows, kv_heads, group_size, HD)

time: 270 us -> 278 us (1.030)
  waiting for transfers between devices: 51 us -> 27.7 us
  local copies, waits for them, and re-layouts: 59.9 us -> 75.7 us
  starting transfers between devices: 0.12 us -> 11.9 us
    all_gather x1 -> x0, waiting for transfers between devices: 24.4 us -> none  [per_device(): lax.all_gather(key_input, 'ctx', axis=0, tiled=True)]
    all_gather x1, waiting for transfers between devices: 21.9 us -> 0.02 us  [per_device(): lax.all_gather(value_input, 'ctx', axis=0, tiled=True)]
    ppermute x0 -> x7, waiting for transfers between devices: none -> 21.8 us  [the longest x4 21.8 us: ring_gather(): lower.append(lax.ppermute(lower[-1] if lower else shard, axis, pairs))]
    ppermute x0 -> x7, starting transfers between devices: none -> 11.8 us  [the longest x3 11.3 us: ring_gather(): upper.append(lax.ppermute(upper[-1] if upper else shard, axis, back))]
    unnamed x22 -> x32, local copies, waits for them, and re-layouts: 10.3 us -> 19.7 us
    gather x0 -> x1, local copies, waits for them, and re-layouts: none -> 3.6 us  [ring_gather(): blocks = blocks[(jnp.arange(size) - shift) % size]]
    reshape x0 -> x1, local copies, waits for them, and re-layouts: none -> 2.85 us  [laid_out(): parts.reshape(*shape[:dim], shape[dim] * shape[dim + 1], *shape[dim + 2:])]
  transfers between devices with their start and end apart: 3 -> 9, of which waited for: 3 -> 4; matrix products, arithmetic and copies ran while one was open for 23% -> 28% of each run, Pallas kernels for 0% -> 0%
where the time goes in v1:
time: 278 us; the launch traced here: 277 us
  matrix products  77.6 us (28%)
  local copies, waits for them, and re-layouts  75.7 us (27%)
  blocking collectives  43.7 us (16%)
  waiting for transfers between devices  27.7 us (10%)
  other arithmetic  25.4 us (9%)
  between operations  14.3 us (5%)
  starting transfers between devices  11.9 us (4%)
    psum x1, blocking collectives, per_device(): sink_grad = lax.psum(partial_sink, ('dp', 'ctx'))  43.7 us
    ppermute x4, waiting for transfers between devices, ring_gather(): lower.append(lax.ppermute(lower[-1] if lower else shard, axis, pairs))  21.8 us
    dot_general x6, matrix products, block_scores(): jnp.einsum('tgrd,ngd->tgrn', query_heads, key_rows, preferred_element_typ...  20.9 us
    unnamed x32, local copies, waits for them, and re-layouts  19.7 us
    dot_general x2, matrix products, advance(): jnp.einsum('tgrn,ngd->tgrd', grad_scores, key_rows, preferred_element_typ...  19.7 us
    dot_general x2, matrix products, advance(): jnp.einsum('tgrn,tgrd->ngd', grad_scores, query_heads, preferred_element_...  15.6 us
    dynamic_slice x10, local copies, waits for them, and re-layouts, key_block(): lax.dynamic_slice_in_dim(table, first_row, block_rows, 0)  12.9 us
    dot_general x2, matrix products, advance(): jnp.einsum('tgrn,ngd->tgrd', weights.astype(jnp.bfloat16), value_rows, pr...  11.4 us
  transfers between devices with their start and end apart: 9, of which 4 were waited for; matrix products, arithmetic and copies ran while one was open for 28% of the time, Pallas kernels for 0%

profile of v1, /device:TPU:0, one launch (start us, length us, event | category | flops | bytes accessed | tf_op | source)
XLA Modules:
  0.0 276.7 jit_solution(9896758427020838751)
XLA Ops:
  7.7 4.1 %collective-permute-start.4 = (bf16[128,1024]{1,0:T(8,128)(2,1)}, bf16[128,1024]{1,0:T(8,128)(2,1)}, u32[]{:S(2)}, u32[]{:S(2)}) collective-permute-start(bf16[128,1024]{1,0:T(8,128)(2,1)} %param.17), channel_id=1, source_target_pairs={{1,0},{2,1},{3,2},{4,3},{5,4},{6,5},{7,6},{0,7},{9,8},{10,9},{11,1... | collective-permute-start | bytes 786440 | tf_op jit(solution)/shard_map/ppermute | solution.py:25
  11.8 1.8 copy.92
  13.7 1.3 fusion.60
  16.7 7.4 %collective-permute-done.1 = bf16[128,1024]{1,0:T(8,128)(2,1)S(1)} collective-permute-done((bf16[128,1024]{1,0:T(8,128)(2,1)S(1)}, bf16[128,1024]{1,0:T(8,128)(2,1)S(1)}, u32[]{:S(2)}, u32[]{:S(2)}) %collective-permute-start.1) | collective-permute-done | bytes 262176 | tf_op jit(solution)/shard_map/ppermute | solution.py:23
  24.9 3.6 %collective-permute-start.5 = (bf16[128,1024]{1,0:T(8,128)(2,1)}, bf16[128,1024]{1,0:T(8,128)(2,1)}, u32[]{:S(2)}, u32[]{:S(2)}) collective-permute-start(bf16[128,1024]{1,0:T(8,128)(2,1)} %collective-permute-done.4), channel_id=1, source_target_pairs={{1,0},{2,1},{3,2},{4,3},{5,4},{6,5},{7,6},{0,7},{9,8},{10,9},{11,1... | collective-permute-start | bytes 786440 | tf_op jit(solution)/shard_map/ppermute | solution.py:25
  28.5 9.2 %collective-permute-done.2 = bf16[128,1024]{1,0:T(8,128)(2,1)} collective-permute-done((bf16[128,1024]{1,0:T(8,128)(2,1)S(1)}, bf16[128,1024]{1,0:T(8,128)(2,1)}, u32[]{:S(2)}, u32[]{:S(2)}) %collective-permute-start.2) | collective-permute-done | bytes 262176 | tf_op jit(solution)/shard_map/ppermute | solution.py:23
  37.9 1.6 copy.94
  41.0 1.3 copy.101
  42.3 3.6 %collective-permute-start.6 = (bf16[128,1024]{1,0:T(8,128)(2,1)}, bf16[128,1024]{1,0:T(8,128)(2,1)S(1)}, u32[]{:S(2)}, u32[]{:S(2)}) collective-permute-start(bf16[128,1024]{1,0:T(8,128)(2,1)} %collective-permute-done.5), channel_id=1, source_target_pairs={{1,0},{2,1},{3,2},{4,3},{5,4},{6,5},{7,6},{0,7},{9,8},{10,9},{11,1... | collective-permute-start | bytes 786440 | tf_op jit(solution)/shard_map/ppermute | solution.py:25
  45.9 5.2 %collective-permute-done.3 = bf16[128,1024]{1,0:T(8,128)(2,1)} collective-permute-done((bf16[128,1024]{1,0:T(8,128)(2,1)}, bf16[128,1024]{1,0:T(8,128)(2,1)}, u32[]{:S(2)}, u32[]{:S(2)}) %collective-permute-start.3) | collective-permute-done | bytes 262176 | tf_op jit(solution)/shard_map/ppermute | solution.py:23
  51.2 1.7 bitcast_dynamic-update-slice_fusion.7
  52.8 1.7 bitcast_dynamic-update-slice_fusion.6
  54.5 1.7 bitcast_dynamic-update-slice_fusion.5
  56.2 1.7 bitcast_dynamic-update-slice_fusion.4
  58.6 1.7 bitcast_dynamic-update-slice_fusion.2
  60.2 1.7 bitcast_dynamic-update-slice_fusion.1
  62.6 3.6 %gather_fusion = bf16[8,128,1024]{2,1,0:T(8,128)(2,1)} fusion(bf16[8,128,1024]{2,1,0:T(8,128)(2,1)} %bitcast_dynamic-update-slice_fusion, s32[1024]{0:T(1024)S(1)} %pad_clamp_fusion), kind=kCustom, calls=%fused_computation | custom fusion | bytes 4194336 | tf_op jit(solution)/shard_map/gather | solution.py:28
  66.2 2.9 %copy.128 = bf16[1024,1024]{0,1:T(8,128)(2,1)S(1)} copy(bf16[1024,1024]{1,0:T(8,128)(2,1)} %bitcast.243) | data formatting | bytes 4194304 | tf_op jit(solution)/shard_map/reshape | solution.py:13
  69.1 7.7 %while.60 = (s32[]{:T(128)}, f32[128,8,4]{0,2,1:T(4,128)S(1)}, f32[128,8,4]{0,2,1:T(4,128)S(1)}, s32[128]{0:T(128)S(1)}, s32[1024]{0:T(1024)S(1)}, /*index=5*/s3...) while((s32[]{:T(128)}, f32[128,8,4]{0,2,1:T(4,128)S(1)}, ...), condition=%wide.region_8.9_spmd.clone, body=%wide.region_5.8_spmd.clone.sunk | while | flops 551759872 | bytes 21394624 | solution.py:63
  69.6 1.5 fusion.120
  71.1 1.8 fusion.121
  73.5 1.5 fusion.120
  75.0 1.8 fusion.121
  76.9 17.6 %while.61 = (s32[]{:T(128)}, f32[128,8,4,128]{0,3,2,1:T(8,128)}, bf16[1024,1024]{0,1:T(8,128)(2,1)}, s32[128]{0:T(128)S(1)}, s32[1024]{0:T(1024)S(1)}, /*index=5...) while((s32[]{:T(128)}, f32[128,8,4,128]{0,3,2,1:T(8,128)}, ...), condition=%wide.region_10.11_spmd.clone, body=%wide.region_9.10_spmd.clone.sunk | while | flops 1085472768 | bytes 11711697 | solution.py:63
  77.3 2.7 constant_dynamic-slice_fusion.15
  80.0 5.3 %bitcast_add_fusion.4 = f32[128,8,4,128]{0,3,2,1:T(8,128)} fusion(f32[128,8,4,128]{0,3,2,1:T(8,128)} %get-tuple-element.1586, bf16[512,8,128,1]{0,2,3,1:T(8,128)(2,1)} %bitcast.240, f32[128,8,4]{0,2,1:T(4,128)S(1)} %get-tuple-element.1610, f32[128,8,4]{0,2,1:T(4,128)S(1)} %get-tuple-element.1609, pred[128,512]{0,1:T(8,128)(4,1)S(1)} %compare_and_fusion.10, ...), kind=kOutput, calls=%fused_computation.40.clone.1 | convolution fusion | flops 1085276160 | bytes 7438337 | tf_op jit(solution)/shard_map/while/body/eval_jaxpr/tgrn,ngd->tgrd/dot_general | solution.py:111
  85.7 2.8 constant_dynamic-slice_fusion.15
  88.5 6.0 %bitcast_add_fusion.4 = f32[128,8,4,128]{0,3,2,1:T(8,128)} fusion(f32[128,8,4,128]{0,3,2,1:T(8,128)} %get-tuple-element.1586, bf16[512,8,128,1]{0,2,3,1:T(8,128)(2,1)} %bitcast.240, f32[128,8,4]{0,2,1:T(4,128)S(1)} %get-tuple-element.1610, f32[128,8,4]{0,2,1:T(4,128)S(1)} %get-tuple-element.1609, pred[128,512]{0,1:T(8,128)(4,1)S(1)} %compare_and_fusion.10, ...), kind=kOutput, calls=%fused_computation.40.clone.1 | convolution fusion | flops 1085276160 | bytes 7438337 | tf_op jit(solution)/shard_map/while/body/eval_jaxpr/tgrn,ngd->tgrd/dot_general | solution.py:111
  94.5 3.3 %multiply_reduce_fusion = (f32[128,8,4]{0,2,1:T(4,128)S(1)}, bf16[128,8,4,128]{0,3,2,1:T(8,128)(2,1)}) fusion(bf16[128,4096]{0,1:T(8,128)(2,1)} %copy-done.7, f32[128,8,4,128]{0,3,2,1:T(8,128)} %get-tuple-element.790), kind=kLoop, calls=%fused_computation.63 | loop fusion | flops 2617344 | bytes 4210688 | tf_op jit(solution)/shard_map/reduce_sum | solution.py:218
  97.8 2.2 broadcast.329.clone
  100.1 2.2 broadcast.329.clone2
  102.3 54.6 %while.59 = (s32[]{:T(128)}, f32[1024,8,128]{2,1,0:T(8,128)}, f32[1024,8,128]{2,1,0:T(8,128)}, s32[128]{0:T(128)S(1)}, s32[1024]{0:T(1024)S(1)}, /*index=5*/s32[...) while((s32[]{:T(128)}, f32[1024,8,128]{2,1,0:T(8,128)}, ...), condition=%wide.region_15.16_spmd, body=%wide.region_14.15_spmd.sunk | while | flops 2166554624 | bytes 132314512 | solution.py:63
  102.8 4.5 %fusion.115 = f32[128,8,4,512]{0,3,2,1:T(8,128)} fusion(f32[128,8,4]{0,2,1:T(4,128)S(1)} %get-tuple-element.1712, f32[128,8,4]{0,2,1:T(4,128)S(1)} %get-tuple-element.1711, pred[128,512]{0,1:T(8,128)(4,1)S(1)} %compare_and_fusion.8, bf16[512,8,128,1]{0,2,3,1:T(8,128)(2,1)S(1)} %bitcast.241, bf16[128,8,4,128]{3,0,2,1:T(8,128)(2,1)S(1)} %get-tuple-element.1710), kind=kOutput, calls=%fused_computation.8.clone.1 | convolution fusion | flops 545259520 | bytes 10584064 | tf_op jit(solution)/shard_map/while/body/eval_jaxpr/tgrd,ngd->tgrn/dot_general | solution.py:74
  107.2 1.1 constant_dynamic-slice_fusion.13
  108.3 7.8 %fusion.117 = f32[512,8,128]{2,0,1:T(8,128)} fusion(bf16[128,8,4,128]{3,0,2,1:T(8,128)(2,1)S(1)} %get-tuple-element.1710, f32[128,8,4,512]{0,3,2,1:T(8,128)} %fusion.115, f32[128,8,4]{0,2,1:T(4,128)S(1)} %get-tuple-element.1715, bf16[512,8,128,1]{0,2,3,1:T(8,128)(2,1)} %bitcast.237, bf16[128,8,4,128]{3,0,2,1:T(8,128)(2,1)} %get-tuple-element.1714), kind=kOutput, calls=%fused_computation.18.clone.1 | convolution fusion | flops 1082130432 | bytes 13647872 | tf_op jit(solution)/shard_map/while/body/eval_jaxpr/tgrn,tgrd->ngd/dot_general | solution.py:173
  116.1 5.0 %fusion.116 = f32[512,8,128]{2,0,1:T(8,128)S(1)} fusion(bf16[128,8,4,128]{3,0,2,1:T(8,128)(2,1)} %get-tuple-element.1714, f32[128,8,4,512]{0,3,2,1:T(8,128)} %fusion.115), kind=kOutput, calls=%fused_computation.17.clone.1 | convolution fusion | flops 538968064 | bytes 11534336 | tf_op jit(solution)/shard_map/while/body/eval_jaxpr/tgrn,tgrd->ngd/dot_general | solution.py:176
  121.6 1.2 copy-done.5
  122.8 2.9 %copy_dynamic-update-slice_fusion.3 = (f32[1024,8,128]{2,1,0:T(8,128)S(1)}, f32[1024,8,128]{2,1,0:T(8,128)S(1)}) fusion(f32[1024,8,128]{2,1,0:T(8,128)S(1)} %copy-done.5, s32[]{:T(128)S(6)} %select_n.195, f32[512,8,128]{2,0,1:T(8,128)S(1)} %fusion.116, f32[1024,8,128]{2,1,0:T(8,128)S(1)} %copy-done.3, f32[512,8,128]{2,0,1:T(8,128)S(1)} %copy-done), kind=kLoop, calls=%fused_computation.15.clone.1 | loop fusion | bytes 8388612 | tf_op jit(solution)/shard_map/while/body/eval_jaxpr/dynamic_update_slice | solution.py:181
  125.7 2.0 copy-done.4
  127.7 1.9 copy-done.6
  130.1 4.5 %fusion.115 = f32[128,8,4,512]{0,3,2,1:T(8,128)} fusion(f32[128,8,4]{0,2,1:T(4,128)S(1)} %get-tuple-element.1712, f32[128,8,4]{0,2,1:T(4,128)S(1)} %get-tuple-element.1711, pred[128,512]{0,1:T(8,128)(4,1)S(1)} %compare_and_fusion.8, bf16[512,8,128,1]{0,2,3,1:T(8,128)(2,1)S(1)} %bitcast.241, bf16[128,8,4,128]{3,0,2,1:T(8,128)(2,1)S(1)} %get-tuple-element.1710), kind=kOutput, calls=%fused_computation.8.clone.1 | convolution fusion | flops 545259520 | bytes 10584064 | tf_op jit(solution)/shard_map/while/body/eval_jaxpr/tgrd,ngd->tgrn/dot_general | solution.py:74
  135.6 7.8 %fusion.117 = f32[512,8,128]{2,0,1:T(8,128)} fusion(bf16[128,8,4,128]{3,0,2,1:T(8,128)(2,1)S(1)} %get-tuple-element.1710, f32[128,8,4,512]{0,3,2,1:T(8,128)} %fusion.115, f32[128,8,4]{0,2,1:T(4,128)S(1)} %get-tuple-element.1715, bf16[512,8,128,1]{0,2,3,1:T(8,128)(2,1)} %bitcast.237, bf16[128,8,4,128]{3,0,2,1:T(8,128)(2,1)} %get-tuple-element.1714), kind=kOutput, calls=%fused_computation.18.clone.1 | convolution fusion | flops 1082130432 | bytes 13647872 | tf_op jit(solution)/shard_map/while/body/eval_jaxpr/tgrn,tgrd->ngd/dot_general | solution.py:173
  143.4 5.0 %fusion.116 = f32[512,8,128]{2,0,1:T(8,128)S(1)} fusion(bf16[128,8,4,128]{3,0,2,1:T(8,128)(2,1)} %get-tuple-element.1714, f32[128,8,4,512]{0,3,2,1:T(8,128)} %fusion.115), kind=kOutput, calls=%fused_computation.17.clone.1 | convolution fusion | flops 538968064 | bytes 11534336 | tf_op jit(solution)/shard_map/while/body/eval_jaxpr/tgrn,tgrd->ngd/dot_general | solution.py:176
  148.9 1.2 copy-done.5
  150.1 2.9 %copy_dynamic-update-slice_fusion.3 = (f32[1024,8,128]{2,1,0:T(8,128)S(1)}, f32[1024,8,128]{2,1,0:T(8,128)S(1)}) fusion(f32[1024,8,128]{2,1,0:T(8,128)S(1)} %copy-done.5, s32[]{:T(128)S(6)} %select_n.195, f32[512,8,128]{2,0,1:T(8,128)S(1)} %fusion.116, f32[1024,8,128]{2,1,0:T(8,128)S(1)} %copy-done.3, f32[512,8,128]{2,0,1:T(8,128)S(1)} %copy-done), kind=kLoop, calls=%fused_computation.15.clone.1 | loop fusion | bytes 8388612 | tf_op jit(solution)/shard_map/while/body/eval_jaxpr/dynamic_update_slice | solution.py:181
  153.0 2.0 copy-done.4
  155.0 1.9 copy-done.6
  156.9 4.9 %stack_reshape.6 = f32[1024,1,1024]{2,0,1:T(8,128)} reshape(f32[1024,8,128]{2,1,0:T(8,128)} %get-tuple-element.792) | data formatting | bytes 8388608 | tf_op jit(solution)/shard_map/stack;reshape | solution.py:229
  161.8 4.9 %stack_reshape.7 = f32[1024,1,1024]{2,0,1:T(8,128)} reshape(f32[1024,8,128]{2,1,0:T(8,128)} %get-tuple-element.793) | data formatting | bytes 8388608 | tf_op jit(solution)/shard_map/stack;reshape | solution.py:229
  166.7 8.4 %pad_maximum_fusion = f32[1024,2,1024]{2,0,1:T(8,128)} fusion(f32[1024,1,1024]{2,0,1:T(8,128)} %stack_reshape.7, f32[1024,1,1024]{2,0,1:T(8,128)} %stack_reshape.6), kind=kLoop, calls=%fused_computation.62 | loop fusion | flops 2097152 | bytes 16777216 | tf_op jit(solution)/shard_map/stack | solution.py:229
  177.9 1.3 multiply_reduce_fusion.1
  179.3 43.7 %psum.7 = f32[32]{0:T(128)} all-reduce(f32[32]{0:T(128)S(1)} %neg.8), channel_id=1, replica_groups=mesh['dp'=4,'ctx'=8] {'dp','ctx'}, use_global_device_ids=true, to_apply=%region_18.19 | all-reduce | flops 32 | bytes 256 | tf_op jit(solution)/shard_map/psum | solution.py:244
  223.0 34.3 %while.62 = (s32[]{:T(128)}, f32[128,8,4,128]{0,3,2,1:T(8,128)}, bf16[1024,1024]{0,1:T(8,128)(2,1)S(1)}, s32[128]{0:T(128)S(1)}, s32[1024]{0:T(1024)S(1)}, /*ind...) while((s32[]{:T(128)}, f32[128,8,4,128]{0,3,2,1:T(8,128)}, ...), condition=%wide.region_13.14_spmd.clone, body=%wide.region_12.13_spmd.clone.sunk | while | flops 1628635136 | bytes 34796796 | solution.py:63
  223.4 2.4 constant_dynamic-slice_fusion.16
  225.8 4.5 %fusion.133 = f32[8,512,128,4]{2,1,3,0:T(8,128)} fusion(bf16[512,8,128,1]{0,2,3,1:T(8,128)(2,1)S(1)} %bitcast.234, bf16[128,8,4,128]{3,0,2,1:T(8,128)(2,1)S(1)} %get-tuple-element.1656), kind=kOutput, calls=%fused_computation.103.clone.1 | convolution fusion | flops 536870912 | bytes 10485760 | tf_op jit(solution)/shard_map/while/body/eval_jaxpr/tgrd,ngd->tgrn/dot_general | solution.py:74
  230.3 9.6 %bitcast_add_fusion.5 = f32[128,8,4,128]{0,3,2,1:T(8,128)} fusion(f32[128,8,4,128]{0,3,2,1:T(8,128)} %get-tuple-element.1633, bf16[512,8,128,1]{0,2,3,1:T(8,128)(2,1)} %bitcast.235, f32[8,512,128,4]{2,1,3,0:T(8,128)} %fusion.133, f32[128,8,4]{0,2,1:T(4,128)S(1)} %get-tuple-element.1661, f32[128,8,4]{0,2,1:T(4,128)S(1)} %get-tuple-element.1658, ...), kind=kOutput, calls=%fused_computation.56.clone.1 | convolution fusion | flops 1091567616 | bytes 15843329 | tf_op jit(solution)/shard_map/while/body/eval_jaxpr/tgrn,ngd->tgrd/dot_general | solution.py:151
  240.2 2.4 constant_dynamic-slice_fusion.16
  242.7 4.5 %fusion.133 = f32[8,512,128,4]{2,1,3,0:T(8,128)} fusion(bf16[512,8,128,1]{0,2,3,1:T(8,128)(2,1)S(1)} %bitcast.234, bf16[128,8,4,128]{3,0,2,1:T(8,128)(2,1)S(1)} %get-tuple-element.1656), kind=kOutput, calls=%fused_computation.103.clone.1 | convolution fusion | flops 536870912 | bytes 10485760 | tf_op jit(solution)/shard_map/while/body/eval_jaxpr/tgrd,ngd->tgrn/dot_general | solution.py:74
  247.2 10.2 %bitcast_add_fusion.5 = f32[128,8,4,128]{0,3,2,1:T(8,128)} fusion(f32[128,8,4,128]{0,3,2,1:T(8,128)} %get-tuple-element.1633, bf16[512,8,128,1]{0,2,3,1:T(8,128)(2,1)} %bitcast.235, f32[8,512,128,4]{2,1,3,0:T(8,128)} %fusion.133, f32[128,8,4]{0,2,1:T(4,128)S(1)} %get-tuple-element.1661, f32[128,8,4]{0,2,1:T(4,128)S(1)} %get-tuple-element.1658, ...), kind=kOutput, calls=%fused_computation.56.clone.1 | convolution fusion | flops 1091567616 | bytes 15843329 | tf_op jit(solution)/shard_map/while/body/eval_jaxpr/tgrn,ngd->tgrd/dot_general | solution.py:151
  257.4 1.8 convert_element_type.55
  259.2 1.3 copy.129
  260.5 1.3 copy.111
  261.8 5.9 %reduce-scatter.2.cloned.1.call-done = f32[128,2,1024]{2,0,1:T(8,128)} async-done(((f32[1024,2,1024]{2,0,1:T(8,128)}), f32[128,2,1024]{2,0,1:T(8,128)}) %reduce-scatter.2.cloned.1.call-update) | async-done | bytes 1048592 | tf_op jit(solution)/shard_map/reduce_scatter | solution.py:228
  267.7 1.3 convert.4
  (116 shorter events, 15.4 us)
Async XLA Ops:
  7.2 33.1 %copy-start.15 = (f32[32]{0:T(128)S(1)}, f32[32]{0:T(128)}, u32[]{:S(2)}) copy-start(f32[32]{0:T(128)} %param.20) | copy-start | bytes 388
  7.2 33.1 %copy-start.9 = (bf16[128,4096]{1,0:T(8,128)(2,1)S(1)}, bf16[128,4096]{1,0:T(8,128)(2,1)}, u32[]{:S(2)}) copy-start(bf16[128,4096]{1,0:T(8,128)(2,1)} %param.19) | copy-start | bytes 3145732
  7.2 69.7 %all-gather.2.cloned.1.call-start = ((), (), s32[]{:S(2)}) async-start(), calls=%async_computation.1 | async-start | bytes 2359296 | tf_op jit(solution)/shard_map/all_gather | solution.py:206
  7.2 9.2 %collective-permute-start = (bf16[128,1024]{1,0:T(8,128)(2,1)}, bf16[128,1024]{1,0:T(8,128)(2,1)S(1)}, u32[]{:S(2)}, u32[]{:S(2)}) collective-permute-start(bf16[128,1024]{1,0:T(8,128)(2,1)} %param.17), channel_id=1, source_target_pairs={{0,1},{1,2},{2,3},{3,4},{4,5},{5,6},{6,7},{7,0},{8,9},{9,10},{10,1... | collective-permute-start | bytes 786440 | tf_op jit(solution)/shard_map/ppermute | solution.py:23
  7.7 17.2 %collective-permute-start.4 = (bf16[128,1024]{1,0:T(8,128)(2,1)}, bf16[128,1024]{1,0:T(8,128)(2,1)}, u32[]{:S(2)}, u32[]{:S(2)}) collective-permute-start(bf16[128,1024]{1,0:T(8,128)(2,1)} %param.17), channel_id=1, source_target_pairs={{1,0},{2,1},{3,2},{4,3},{5,4},{6,5},{7,6},{0,7},{9,8},{10,9},{11,1... | collective-permute-start | bytes 786440 | tf_op jit(solution)/shard_map/ppermute | solution.py:25
  13.7 254.0 %reduce-scatter.2.cloned.1.call-start = ((), (), s32[]{:S(2)}) async-start(), calls=%async_computation.2 | async-start | bytes 9437184 | tf_op jit(solution)/shard_map/reduce_scatter | solution.py:228
  16.4 23.1 %copy-start.11 = (bf16[128,1024]{1,0:T(8,128)(2,1)}, bf16[128,1024]{1,0:T(8,128)(2,1)S(1)}, u32[]{:S(2)}) copy-start(bf16[128,1024]{1,0:T(8,128)(2,1)S(1)} %collective-permute-done) | copy-start | bytes 786436
  16.5 7.7 %collective-permute-start.1 = (bf16[128,1024]{1,0:T(8,128)(2,1)S(1)}, bf16[128,1024]{1,0:T(8,128)(2,1)S(1)}, u32[]{:S(2)}, u32[]{:S(2)}) collective-permute-start(bf16[128,1024]{1,0:T(8,128)(2,1)S(1)} %collective-permute-done), channel_id=1, source_target_pairs={{0,1},{1,2},{2,3},{3,4},{4,5},{5,6},{6,7},{7,0},{8,9},{9,10},{10,1... | collective-permute-start | bytes 786440 | tf_op jit(solution)/shard_map/ppermute | solution.py:23
  24.1 15.4 %copy-start.12 = (bf16[128,1024]{1,0:T(8,128)(2,1)}, bf16[128,1024]{1,0:T(8,128)(2,1)S(1)}, u32[]{:S(2)}) copy-start(bf16[128,1024]{1,0:T(8,128)(2,1)S(1)} %collective-permute-done.1) | copy-start | bytes 786436
  24.1 13.5 %collective-permute-start.2 = (bf16[128,1024]{1,0:T(8,128)(2,1)S(1)}, bf16[128,1024]{1,0:T(8,128)(2,1)}, u32[]{:S(2)}, u32[]{:S(2)}) collective-permute-start(bf16[128,1024]{1,0:T(8,128)(2,1)S(1)} %collective-permute-done.1), channel_id=1, source_target_pairs={{0,1},{1,2},{2,3},{3,4},{4,5},{5,6},{6,7},{7,0},{8,9},{9,10},{10,1... | collective-permute-start | bytes 786440 | tf_op jit(solution)/shard_map/ppermute | solution.py:23
  24.9 17.4 %collective-permute-start.5 = (bf16[128,1024]{1,0:T(8,128)(2,1)}, bf16[128,1024]{1,0:T(8,128)(2,1)}, u32[]{:S(2)}, u32[]{:S(2)}) collective-permute-start(bf16[128,1024]{1,0:T(8,128)(2,1)} %collective-permute-done.4), channel_id=1, source_target_pairs={{1,0},{2,1},{3,2},{4,3},{5,4},{6,5},{7,6},{0,7},{9,8},{10,9},{11,1... | collective-permute-start | bytes 786440 | tf_op jit(solution)/shard_map/ppermute | solution.py:25
  37.6 13.5 %collective-permute-start.3 = (bf16[128,1024]{1,0:T(8,128)(2,1)}, bf16[128,1024]{1,0:T(8,128)(2,1)}, u32[]{:S(2)}, u32[]{:S(2)}) collective-permute-start(bf16[128,1024]{1,0:T(8,128)(2,1)} %collective-permute-done.2), channel_id=1, source_target_pairs={{0,1},{1,2},{2,3},{3,4},{4,5},{5,6},{6,7},{7,0},{8,9},{9,10},{10,1... | collective-permute-start | bytes 786440 | tf_op jit(solution)/shard_map/ppermute | solution.py:23
  39.5 18.3 %copy-start.10 = (bf16[128,1024]{1,0:T(8,128)(2,1)S(1)}, bf16[128,1024]{1,0:T(8,128)(2,1)}, u32[]{:S(2)}) copy-start(bf16[128,1024]{1,0:T(8,128)(2,1)} %param.17) | copy-start | bytes 786436
  40.3 28.7 %copy-start.13 = (f32[8,4]{1,0:T(8,128)}, f32[8,4]{1,0:T(8,128)S(1)}, u32[]{:S(2)}) copy-start(f32[8,4]{1,0:T(8,128)S(1)} %broadcast_in_dim.234) | copy-start | bytes 388
  41.0 25.2 %copy-start.7 = (bf16[128,4096]{0,1:T(8,128)(2,1)}, bf16[128,4096]{0,1:T(8,128)(2,1)S(1)}, u32[]{:S(2)}) copy-start(bf16[128,4096]{0,1:T(8,128)(2,1)S(1)} %copy.98) | copy-start | bytes 3145732
  42.3 19.5 %collective-permute-start.6 = (bf16[128,1024]{1,0:T(8,128)(2,1)}, bf16[128,1024]{1,0:T(8,128)(2,1)S(1)}, u32[]{:S(2)}, u32[]{:S(2)}) collective-permute-start(bf16[128,1024]{1,0:T(8,128)(2,1)} %collective-permute-done.5), channel_id=1, source_target_pairs={{1,0},{2,1},{3,2},{4,3},{5,4},{6,5},{7,6},{0,7},{9,8},{10,9},{11,1... | collective-permute-start | bytes 786440 | tf_op jit(solution)/shard_map/ppermute | solution.py:25
  102.7 4.5 %copy-start.1 = (bf16[1024,1024]{0,1:T(8,128)(2,1)S(1)}, bf16[1024,1024]{0,1:T(8,128)(2,1)}, u32[]{:S(2)}) copy-start(bf16[1024,1024]{0,1:T(8,128)(2,1)} %get-tuple-element.1713) | copy-start | bytes 6291460 | tf_op jit(solution)/shard_map/while
  116.1 5.0 %copy-start = (f32[512,8,128]{2,0,1:T(8,128)S(1)}, f32[512,8,128]{2,0,1:T(8,128)}, u32[]{:S(2)}) copy-start(f32[512,8,128]{2,0,1:T(8,128)} %fusion.117) | copy-start | bytes 6291460 | tf_op jit(solution)/shard_map/while
  116.1 5.5 %copy-start.3 = (f32[1024,8,128]{2,1,0:T(8,128)S(1)}, f32[1024,8,128]{2,1,0:T(8,128)}, u32[]{:S(2)}) copy-start(f32[1024,8,128]{2,1,0:T(8,128)} %get-tuple-element.1685) | copy-start | bytes 12582916 | tf_op jit(solution)/shard_map/while
  116.1 6.7 %copy-start.5 = (f32[1024,8,128]{2,1,0:T(8,128)S(1)}, f32[1024,8,128]{2,1,0:T(8,128)}, u32[]{:S(2)}) copy-start(f32[1024,8,128]{2,1,0:T(8,128)} %get-tuple-element.1686) | copy-start | bytes 12582916 | tf_op jit(solution)/shard_map/while
  125.7 2.0 copy-start.4
  127.7 1.9 copy-start.6
  130.1 4.5 %copy-start.1 = (bf16[1024,1024]{0,1:T(8,128)(2,1)S(1)}, bf16[1024,1024]{0,1:T(8,128)(2,1)}, u32[]{:S(2)}) copy-start(bf16[1024,1024]{0,1:T(8,128)(2,1)} %get-tuple-element.1713) | copy-start | bytes 6291460 | tf_op jit(solution)/shard_map/while
  143.4 5.0 %copy-start = (f32[512,8,128]{2,0,1:T(8,128)S(1)}, f32[512,8,128]{2,0,1:T(8,128)}, u32[]{:S(2)}) copy-start(f32[512,8,128]{2,0,1:T(8,128)} %fusion.117) | copy-start | bytes 6291460 | tf_op jit(solution)/shard_map/while
  143.4 5.5 %copy-start.3 = (f32[1024,8,128]{2,1,0:T(8,128)S(1)}, f32[1024,8,128]{2,1,0:T(8,128)}, u32[]{:S(2)}) copy-start(f32[1024,8,128]{2,1,0:T(8,128)} %get-tuple-element.1685) | copy-start | bytes 12582916 | tf_op jit(solution)/shard_map/while
  143.4 6.7 %copy-start.5 = (f32[1024,8,128]{2,1,0:T(8,128)S(1)}, f32[1024,8,128]{2,1,0:T(8,128)}, u32[]{:S(2)}) copy-start(f32[1024,8,128]{2,1,0:T(8,128)} %get-tuple-element.1686) | copy-start | bytes 12582916 | tf_op jit(solution)/shard_map/while
  153.0 2.0 copy-start.4
  155.0 1.9 copy-start.6
  175.0 0.7 copy-start.14
  225.8 4.5 %copy-start.2 = (bf16[512,1024]{0,1:T(8,128)(2,1)}, bf16[512,1024]{0,1:T(8,128)(2,1)S(1)}, u32[]{:S(2)}) copy-start(bf16[512,1024]{0,1:T(8,128)(2,1)S(1)} %get-tuple-element.1529) | copy-start | bytes 3145732 | tf_op jit(solution)/shard_map/while
  242.7 4.5 %copy-start.2 = (bf16[512,1024]{0,1:T(8,128)(2,1)}, bf16[512,1024]{0,1:T(8,128)(2,1)S(1)}, u32[]{:S(2)}) copy-start(bf16[512,1024]{0,1:T(8,128)(2,1)S(1)} %get-tuple-element.1529) | copy-start | bytes 3145732 | tf_op jit(solution)/shard_map/while
  257.4 3.2 %copy-start.8 = (bf16[128,8,4,128]{0,3,2,1:T(8,128)(2,1)S(1)}, bf16[128,8,4,128]{0,3,2,1:T(8,128)(2,1)}, u32[]{:S(2)}) copy-start(bf16[128,8,4,128]{0,3,2,1:T(8,128)(2,1)} %get-tuple-element.1216) | copy-start | bytes 3145732
Sparse Core Ops, SparseCore 0:
  13.8 39.6 all-gather.1
  175.2 92.4 reduce-scatter.1
